TPU v7x, 32 devices: a whole 2x2x4 slice. The times are simulated.
32 devices in a mesh: grp: 4 (over z), tile: 8 (over y, x, core).
Axes of the slice: x: 2, y: 2, z: 4, core: 2. Of those that a mesh axis runs over, the one named last changes fastest.
Arguments:
- right_side: float32 [16, 32768], P(None, ('grp', 'tile')), may hold values from -6 to 6
- ridge: float32 [32768], P(('grp', 'tile')), may hold values from 1 to 4
- tiles: float32 [128, 1024, 1024], P(('grp', 'tile')), may hold values from -0.013671875 to 0.013671875
- tile_list: int32 [128, 2], P(('grp', 'tile')), may hold values from 0 to 31, as said below
Outputs:
- solution: float32 [16, 32768], P(None, ('grp', 'tile'))
- residual: float32 [16, 32768], P(None, ('grp', 'tile'))
Inputs may be any that keep to these rules, and one draw needn't show every extreme that they name: `tile_list`: each row is a pair (row block, column block) with row block >= column block; no pair appears twice; rows stand in packed row-major order (row block rising, then column block rising).
All inputs are finite; a program needn't handle non-finite values.
Results may differ from a plain program's by a relative error of at most 0.0003.
Values sent between devices are 32-bit elements; how exact they have to be, the bound alone decides.
A program may use at most 64 MiB of HBM per device.

v0:
```python
import jax
import jax.numpy as jnp
from jax import lax
from jax.sharding import PartitionSpec as P

ITERS = 2


def gauss_solve(matrix, rhs):
    order = matrix.shape[0]
    for pivot in range(order):
        scale = 1.0 / matrix[pivot, pivot]
        row_new = matrix[pivot] * scale
        rhs_new = rhs[pivot] * scale
        factor = matrix[:, pivot] * (1.0 - (jnp.arange(order) == pivot).astype(matrix.dtype))
        matrix = matrix - factor[:, None] * row_new[None, :]
        rhs = rhs - factor[:, None] * rhs_new[None, :]
        matrix = matrix.at[pivot].set(row_new)
        rhs = rhs.at[pivot].set(rhs_new)
    return rhs


def gram(left, right):
    return lax.dot_general(
        left,
        right,
        (((1,), (1,)), ((), ())),
        precision=lax.Precision.HIGHEST,
        preferred_element_type=jnp.float32,
    )


def mixed(coeffs, rows):
    return jnp.dot(coeffs.T, rows, precision=lax.Precision.HIGHEST)


def tile_masks(order):
    rowid = lax.broadcasted_iota(jnp.int32, (order, order), 0)
    colid = lax.broadcasted_iota(jnp.int32, (order, order), 1)
    return (rowid >= colid, rowid > colid)


def apply_kernel(tiles, tile_list, field):
    order = tiles.shape[1]
    lower, strict = tile_masks(order)

    def step(total, item):
        tile, pair = item
        block_row = pair[0]
        block_col = pair[1]
        differ = block_row != block_col
        direct_tile = jnp.where(jnp.logical_or(lower, differ), tile, jnp.zeros_like(tile))
        mirror_tile = jnp.where(jnp.logical_or(strict, differ), tile, jnp.zeros_like(tile))
        row_start = block_row * order
        col_start = block_col * order
        from_col = lax.dynamic_slice_in_dim(field, col_start, order, 1)
        from_row = lax.dynamic_slice_in_dim(field, row_start, order, 1)
        into_row = lax.dot_general(
            from_col,
            direct_tile,
            (((1,), (1,)), ((), ())),
            precision=lax.Precision.HIGHEST,
            preferred_element_type=jnp.float32,
        )
        into_col = jnp.dot(
            from_row,
            mirror_tile,
            precision=lax.Precision.HIGHEST,
            preferred_element_type=jnp.float32,
        )
        total = lax.dynamic_update_slice_in_dim(
            total, lax.dynamic_slice_in_dim(total, row_start, order, 1) + into_row, row_start, 1
        )
        total = lax.dynamic_update_slice_in_dim(
            total, lax.dynamic_slice_in_dim(total, col_start, order, 1) + into_col, col_start, 1
        )
        return (total, None)

    start = jnp.zeros(field.shape, jnp.float32)
    total, _ = lax.scan(step, start, (tiles, tile_list))
    return total


def local(right_side, ridge, tiles, tile_list):
    local_width = right_side.shape[1]
    whole_rhs, whole_ridge = (
        lax.all_gather(right_side, ("grp", "tile"), axis=1, tiled=True),
        lax.all_gather(ridge, ("grp", "tile"), axis=0, tiled=True),
    )
    solution = jnp.zeros_like(whole_rhs)
    residual = whole_rhs
    direction = whole_rhs
    norm_now = gram(residual, residual)
    for step in range(ITERS):
        partial_image = apply_kernel(tiles, tile_list, direction)
        image = lax.psum(partial_image, ("grp", "tile")) + whole_ridge[None, :] * direction
        alpha = gauss_solve(gram(direction, image), norm_now)
        solution = solution + mixed(alpha, direction)
        residual = residual - mixed(alpha, image)
        if step + 1 < ITERS:
            norm_next = gram(residual, residual)
            beta = gauss_solve(norm_now, norm_next)
            direction = residual + mixed(beta, direction)
            norm_now = norm_next
    offset = lax.axis_index(("grp", "tile")) * local_width
    solution = lax.dynamic_slice_in_dim(solution, offset, local_width, 1)
    residual = lax.dynamic_slice_in_dim(residual, offset, local_width, 1)
    return (solution, residual)


def solution(mesh):
    return jax.shard_map(
        local,
        mesh=mesh,
        in_specs=(
            P(None, ("grp", "tile")),
            P(("grp", "tile")),
            P(("grp", "tile"), None, None),
            P(("grp", "tile"), None),
        ),
        out_specs=(P(None, ("grp", "tile")), P(None, ("grp", "tile"))),
        check_vma=False,
    )
```

profile of v0, /device:TPU:0, one launch (start us, length us, event | category | flops | bytes accessed | tf_op | source)
XLA Modules:
  0.0 568.2 jit_solution(14640766748409336953)
XLA Ops:
  7.2 0.7 all-gather.2.cloned.1.call-update
  8.0 62.1 %all-gather.2.cloned.1.call-done = f32[16,32768]{1,0:T(8,128)} async-done(((f32[16,1024]{1,0:T(8,128)}), f32[16,32768]{1,0:T(8,128)}) %all-gather.2.cloned.1.call-update) | async-done | bytes 2097168 | tf_op jit(solution)/shard_map/all_gather | solution.py:87
  70.1 1.4 broadcast.1560.clone
  71.5 0.9 copy-done
  72.4 57.3 %while.115 = (s32[]{:T(128)}, f32[16,32768]{1,0:T(8,128)}, s32[4,2]{0,1:T(2,128)S(1)}, f32[16,32768]{1,0:T(8,128)S(1)}, f32[4,1024,1024]{2,1,0:T(8,128)}, /*inde...) while((s32[]{:T(128)}, f32[16,32768]{1,0:T(8,128)}, s32[4,2]{0,1:T(2,128)S(1)}, ...), condition=%wide.region_1.2_spmd.clone, body=%wide.region_0.1_spmd.clone.sunk | while | flops 408977408 | bytes 8783110 | solution.py:80
  75.4 6.2 %fusion.231 = f32[16,32768]{1,0:T(8,128)} fusion(f32[16,32768]{1,0:T(8,128)} %get-tuple-element.1416, s32[]{:T(128)S(6)} %select_n.80, f32[4,1024,1024]{2,1,0:T(8,128)} %get-tuple-element.1428, s32[]{:T(128)S(6)} %copy.29, pred[]{:T(512)} %bitcast.292, f32[16,32768]{1,0:T(8,128)S(1)} %get-tuple-element.1427, s32[]{:T(128)S(6)} %select_n.81), kind=kOutput, calls=%fused_computation.21.clone.1 | convolution fusion | flops 204488704 | bytes 4391436 | tf_op jit(solution)/shard_map/while/body/eval_jaxpr/dot_general | solution.py:58
  81.7 5.1 fusion.232
  89.8 6.2 %fusion.231 = f32[16,32768]{1,0:T(8,128)} fusion(f32[16,32768]{1,0:T(8,128)} %get-tuple-element.1416, s32[]{:T(128)S(6)} %select_n.80, f32[4,1024,1024]{2,1,0:T(8,128)} %get-tuple-element.1428, s32[]{:T(128)S(6)} %copy.29, pred[]{:T(512)} %bitcast.292, f32[16,32768]{1,0:T(8,128)S(1)} %get-tuple-element.1427, s32[]{:T(128)S(6)} %select_n.81), kind=kOutput, calls=%fused_computation.21.clone.1 | convolution fusion | flops 204488704 | bytes 4391436 | tf_op jit(solution)/shard_map/while/body/eval_jaxpr/dot_general | solution.py:58
  96.0 5.1 fusion.232
  104.1 6.2 %fusion.231 = f32[16,32768]{1,0:T(8,128)} fusion(f32[16,32768]{1,0:T(8,128)} %get-tuple-element.1416, s32[]{:T(128)S(6)} %select_n.80, f32[4,1024,1024]{2,1,0:T(8,128)} %get-tuple-element.1428, s32[]{:T(128)S(6)} %copy.29, pred[]{:T(512)} %bitcast.292, f32[16,32768]{1,0:T(8,128)S(1)} %get-tuple-element.1427, s32[]{:T(128)S(6)} %select_n.81), kind=kOutput, calls=%fused_computation.21.clone.1 | convolution fusion | flops 204488704 | bytes 4391436 | tf_op jit(solution)/shard_map/while/body/eval_jaxpr/dot_general | solution.py:58
  110.3 5.1 fusion.232
  118.4 6.2 %fusion.231 = f32[16,32768]{1,0:T(8,128)} fusion(f32[16,32768]{1,0:T(8,128)} %get-tuple-element.1416, s32[]{:T(128)S(6)} %select_n.80, f32[4,1024,1024]{2,1,0:T(8,128)} %get-tuple-element.1428, s32[]{:T(128)S(6)} %copy.29, pred[]{:T(512)} %bitcast.292, f32[16,32768]{1,0:T(8,128)S(1)} %get-tuple-element.1427, s32[]{:T(128)S(6)} %select_n.81), kind=kOutput, calls=%fused_computation.21.clone.1 | convolution fusion | flops 204488704 | bytes 4391436 | tf_op jit(solution)/shard_map/while/body/eval_jaxpr/dot_general | solution.py:58
  124.7 5.1 fusion.232
  129.8 0.6 copy-done.5
  130.4 40.1 %all_gather.7 = f32[32768]{0:T(1024)S(1)} all-gather(f32[1024]{0:T(1024)S(1)} %copy-done.5), channel_id=1, replica_groups=mesh['grp'=4,'tile'=8] {'grp','tile'}, dimensions={0}, use_global_device_ids=true | all-gather | bytes 135168 | tf_op jit(solution)/shard_map/all_gather | solution.py:88
  170.5 2.9 fusion.110
  174.8 88.8 %all-reduce.3.cloned.1.call-done = f32[16,32768]{1,0:T(8,128)} async-done(((f32[16,32768]{1,0:T(8,128)}), f32[16,32768]{1,0:T(8,128)}) %all-reduce.3.cloned.1.call-update) | async-done | bytes 2097168 | tf_op jit(solution)/shard_map/psum | solution.py:96
  263.6 4.5 fusion.55
  269.6 0.6 slice.2233
  271.1 0.6 slice.2171
  272.7 0.6 slice.2175
  274.3 0.6 slice.2179
  276.0 0.6 slice.2183
  277.6 0.6 slice.2187
  279.2 0.6 slice.2191
  280.8 0.6 slice.2195
  282.4 0.6 slice.2199
  284.1 0.6 slice.2203
  285.7 0.6 slice.2207
  287.3 0.6 slice.2211
  288.9 0.6 slice.2215
  290.7 0.6 slice.2219
  292.4 0.6 slice.2223
  294.0 0.6 slice.2227
  295.6 3.6 convolution_subtract_fusion
  299.2 2.8 fusion.112
  325.2 4.3 convolution_add_fusion
  329.5 1.5 broadcast.1560
  331.0 57.8 %while.116 = (s32[]{:T(128)}, f32[16,32768]{1,0:T(8,128)}, s32[4,2]{0,1:T(2,128)S(1)}, f32[16,32768]{1,0:T(8,128)}, f32[4,1024,1024]{2,1,0:T(8,128)}, /*index=5*/s32[]{:T(128)}, s32[1,1]{0,1:T(1,128)}, s32[]{:T(128)}, s32[]{:T(128)}) while((s32[]{:T(128)}, f32[16,32768]{1,0:T(8,128)}, s32[4,2]{0,1:T(2,128)S(1)}, ...), condition=%wide.region_4.5_spmd.clone, body=%wide.region_3.4_spmd.clone.sunk | while | flops 408977408 | bytes 8783110 | solution.py:80
  334.2 6.2 %fusion.236 = f32[16,32768]{1,0:T(8,128)} fusion(f32[16,32768]{1,0:T(8,128)} %get-tuple-element.1443, s32[]{:T(128)S(6)} %select_n.84, f32[4,1024,1024]{2,1,0:T(8,128)} %get-tuple-element.1455, s32[]{:T(128)S(6)} %copy.98, pred[]{:T(512)} %bitcast.297, f32[16,32768]{1,0:T(8,128)} %get-tuple-element.1454, s32[]{:T(128)S(6)} %select_n.85), kind=kOutput, calls=%fused_computation.46.clone.1 | convolution fusion | flops 204488704 | bytes 4391436 | tf_op jit(solution)/shard_map/while/body/eval_jaxpr/dot_general | solution.py:58
  340.4 5.1 fusion.237
  348.6 6.2 %fusion.236 = f32[16,32768]{1,0:T(8,128)} fusion(f32[16,32768]{1,0:T(8,128)} %get-tuple-element.1443, s32[]{:T(128)S(6)} %select_n.84, f32[4,1024,1024]{2,1,0:T(8,128)} %get-tuple-element.1455, s32[]{:T(128)S(6)} %copy.98, pred[]{:T(512)} %bitcast.297, f32[16,32768]{1,0:T(8,128)} %get-tuple-element.1454, s32[]{:T(128)S(6)} %select_n.85), kind=kOutput, calls=%fused_computation.46.clone.1 | convolution fusion | flops 204488704 | bytes 4391436 | tf_op jit(solution)/shard_map/while/body/eval_jaxpr/dot_general | solution.py:58
  354.9 5.1 fusion.237
  363.1 6.2 %fusion.236 = f32[16,32768]{1,0:T(8,128)} fusion(f32[16,32768]{1,0:T(8,128)} %get-tuple-element.1443, s32[]{:T(128)S(6)} %select_n.84, f32[4,1024,1024]{2,1,0:T(8,128)} %get-tuple-element.1455, s32[]{:T(128)S(6)} %copy.98, pred[]{:T(512)} %bitcast.297, f32[16,32768]{1,0:T(8,128)} %get-tuple-element.1454, s32[]{:T(128)S(6)} %select_n.85), kind=kOutput, calls=%fused_computation.46.clone.1 | convolution fusion | flops 204488704 | bytes 4391436 | tf_op jit(solution)/shard_map/while/body/eval_jaxpr/dot_general | solution.py:58
  369.3 5.1 fusion.237
  377.5 6.2 %fusion.236 = f32[16,32768]{1,0:T(8,128)} fusion(f32[16,32768]{1,0:T(8,128)} %get-tuple-element.1443, s32[]{:T(128)S(6)} %select_n.84, f32[4,1024,1024]{2,1,0:T(8,128)} %get-tuple-element.1455, s32[]{:T(128)S(6)} %copy.98, pred[]{:T(512)} %bitcast.297, f32[16,32768]{1,0:T(8,128)} %get-tuple-element.1454, s32[]{:T(128)S(6)} %select_n.85), kind=kOutput, calls=%fused_computation.46.clone.1 | convolution fusion | flops 204488704 | bytes 4391436 | tf_op jit(solution)/shard_map/while/body/eval_jaxpr/dot_general | solution.py:58
  383.7 5.1 fusion.237
  388.8 3.2 fusion.111
  392.1 130.4 %all-reduce.5.cloned.1.call-done = f32[16,32768]{1,0:T(8,128)} async-done(((f32[16,32768]{1,0:T(8,128)}), f32[16,32768]{1,0:T(8,128)}) %all-reduce.5.cloned.1.call-update) | async-done | bytes 2097168 | tf_op jit(solution)/shard_map/psum | solution.py:96
  522.5 5.8 %fusion.54 = f32[16,16]{1,0:T(8,128)S(1)} fusion(f32[16,32768]{1,0:T(8,128)} %get-tuple-element.1465, f32[16,32768]{1,0:T(8,128)} %all-reduce.5.cloned.1.call-done, f32[32768]{0:T(1024)S(1)} %all_gather.7), kind=kOutput, calls=%fused_computation.60 | convolution fusion | flops 101711872 | bytes 4326400 | tf_op jit(solution)/shard_map/dot_general | solution.py:24
  529.8 0.6 slice.2295
  533.1 0.6 slice.2303
  534.8 0.6 slice.2307
  536.4 0.6 slice.2311
  538.1 0.6 slice.2315
  539.7 0.6 slice.2319
  543.0 0.6 slice.2327
  544.7 0.6 slice.2331
  548.2 0.6 slice.2339
  549.9 0.6 slice.2343
  554.8 1.9 fusion.113
  556.8 2.0 fusion.53
  558.7 1.5 dynamic-slice_subtract_fusion
  560.2 1.5 dynamic-slice_add_fusion
  (423 shorter events, 34.2 us)
Async XLA Ops:
  7.2 64.3 %copy-start.4 = (s32[4,2]{0,1:T(2,128)S(1)}, s32[4,2]{0,1:T(2,128)}, u32[]{:S(2)}) copy-start(s32[4,2]{0,1:T(2,128)} %param.197) | copy-start | bytes 100
  7.2 62.9 %all-gather.2.cloned.1.call-start = ((), (), s32[]{:S(2)}) async-start(), calls=%async_computation | async-start | bytes 2162688 | tf_op jit(solution)/shard_map/all_gather | solution.py:87
  7.9 255.7 %all-reduce.3.cloned.1.call-start = ((), (), s32[]{:S(2)}) async-start(), calls=%async_computation.1 | async-start | bytes 4194304 | tf_op jit(solution)/shard_map/psum | solution.py:96
  70.1 2.3 copy-start
  129.7 0.7 copy-start.5
  129.8 392.8 %all-reduce.5.cloned.1.call-start = ((), (), s32[]{:S(2)}) async-start(), calls=%async_computation.2 | async-start | bytes 4194304 | tf_op jit(solution)/shard_map/psum | solution.py:96
  299.2 2.8 copy-start.2
  522.5 32.3 %copy-start.1 = (f32[16,32768]{1,0:T(8,128)S(1)}, f32[16,32768]{1,0:T(8,128)}, u32[]{:S(2)}) copy-start(f32[16,32768]{1,0:T(8,128)} %get-tuple-element.1465) | copy-start | bytes 6291460
  554.8 1.9 copy-start.3
Sparse Core Ops, SparseCore 0:
  10.9 59.1 all-gather.1
  129.9 133.6 all-reduce.2
  389.0 133.5 all-reduce.4
where the time goes:
time: 569 us; the launch traced here: 568 us
  waiting for transfers between devices  282 us (50%)
  matrix products  122 us (21%)
  between operations  47.7 us (8%)
  local copies, waits for them, and re-layouts  40.6 us (7%)
  blocking collectives  40.1 us (7%)
  loops' own time  19.8 us (3%)
  other arithmetic  16.3 us (3%)
    psum x2, waiting for transfers between devices, local(): lax.psum(partial_image, ('grp', 'tile')) + whole_ridge[None, :] * direction  219 us
    all_gather x1, waiting for transfers between devices, local(): lax.all_gather(right_side, ('grp', 'tile'), axis=1, tiled=True)  62.1 us
    dot_general x8, matrix products, step(): lax.dot_general(from_col, direct_tile, (((1,), (1,)), ((), ())), precisio...  49.9 us
    dot_general x8, matrix products, step(): jnp.dot(from_row, mirror_tile, precision=lax.Precision.HIGHEST, preferred...  40.6 us
    all_gather x1, blocking collectives, local(): lax.all_gather(ridge, ('grp', 'tile'), axis=0, tiled=True)  40.1 us
    slice x48, local copies, waits for them, and re-layouts, gauss_solve(): scale = 1.0 / matrix[pivot, pivot]  28.1 us
    another operation x2, loops' own time, apply_kernel(): total, _ = lax.scan(step, start, (tiles, tile_list))  19.8 us
    dot_general x4, matrix products, gram(): lax.dot_general(left, right, (((1,), (1,)), ((), ())), precision=lax.Prec...  16.1 us
  transfers between devices with their start and end apart: 3, of which 3 were waited for; matrix products, arithmetic and copies ran while one was open for 1% of the time, Pallas kernels for 0%

commit v1 on v0

--- a/solution.py
+++ b/solution.py
@@ -4,6 +4,11 @@
 from jax.sharding import PartitionSpec as P
 
 ITERS = 2
+
+
+def by_each_axis(array, axis_one, axis_two):
+    inner = lax.psum(array, axis_one)
+    return lax.psum(inner, axis_two)
 
 
 def gauss_solve(matrix, rhs):
@@ -93,7 +98,7 @@
     norm_now = gram(residual, residual)
     for step in range(ITERS):
         partial_image = apply_kernel(tiles, tile_list, direction)
-        image = lax.psum(partial_image, ("grp", "tile")) + whole_ridge[None, :] * direction
+        image = by_each_axis(partial_image, "tile", "grp") + whole_ridge[None, :] * direction
         alpha = gauss_solve(gram(direction, image), norm_now)
         solution = solution + mixed(alpha, direction)
         residual = residual - mixed(alpha, image)

time: 569 us -> 600 us (1.054)
  waiting for transfers between devices: 282 us -> 311 us
    psum x2 -> x4, waiting for transfers between devices: 219 us -> 248 us  [the longest x2 126 us: by_each_axis(): return lax.psum(inner, axis_two)]
  transfers between devices with their start and end apart: 3 -> 5, of which waited for: 3 -> 5; matrix products, arithmetic and copies ran while one was open for 1% -> 1% of each run, Pallas kernels for 0% -> 0%
where the time goes in v1:
time: 600 us; the launch traced here: 599 us
  waiting for transfers between devices  311 us (52%)
  matrix products  122 us (20%)
  between operations  47.8 us (8%)
  blocking collectives  42 us (7%)
  local copies, waits for them, and re-layouts  40 us (7%)
  loops' own time  20.4 us (3%)
  other arithmetic  16.3 us (3%)
    psum x2, waiting for transfers between devices, by_each_axis(): return lax.psum(inner, axis_two)  126 us
    psum x2, waiting for transfers between devices, by_each_axis(): inner = lax.psum(array, axis_one)  122 us
    all_gather x1, waiting for transfers between devices, local(): lax.all_gather(right_side, ('grp', 'tile'), axis=1, tiled=True)  62.1 us
    dot_general x8, matrix products, step(): lax.dot_general(from_col, direct_tile, (((1,), (1,)), ((), ())), precisio...  49.9 us
    all_gather x1, blocking collectives, local(): lax.all_gather(ridge, ('grp', 'tile'), axis=0, tiled=True)  42 us
    dot_general x8, matrix products, step(): jnp.dot(from_row, mirror_tile, precision=lax.Precision.HIGHEST, preferred...  40.6 us
    slice x48, local copies, waits for them, and re-layouts, gauss_solve(): scale = 1.0 / matrix[pivot, pivot]  28.1 us
    another operation x2, loops' own time, apply_kernel(): total, _ = lax.scan(step, start, (tiles, tile_list))  20.4 us
  transfers between devices with their start and end apart: 5, of which 5 were waited for; matrix products, arithmetic and copies ran while one was open for 1% of the time, Pallas kernels for 0%

profile of v1, /device:TPU:0, one launch (start us, length us, event | category | flops | bytes accessed | tf_op | source)
XLA Modules:
  0.0 598.9 jit_solution(11250268382562658993)
XLA Ops:
  7.2 0.7 all-gather.2.cloned.1.call-update
  8.0 62.1 %all-gather.2.cloned.1.call-done = f32[16,32768]{1,0:T(8,128)} async-done(((f32[16,1024]{1,0:T(8,128)}), f32[16,32768]{1,0:T(8,128)}) %all-gather.2.cloned.1.call-update) | async-done | bytes 2097168 | tf_op jit(solution)/shard_map/all_gather | solution.py:92
  70.1 1.5 broadcast.1560.clone
  71.6 0.9 copy-done
  72.4 57.8 %while.115 = (s32[]{:T(128)}, f32[16,32768]{1,0:T(8,128)}, s32[4,2]{0,1:T(2,128)S(1)}, f32[16,32768]{1,0:T(8,128)S(1)}, f32[4,1024,1024]{2,1,0:T(8,128)}, /*inde...) while((s32[]{:T(128)}, f32[16,32768]{1,0:T(8,128)}, s32[4,2]{0,1:T(2,128)S(1)}, ...), condition=%wide.region_1.2_spmd.clone, body=%wide.region_0.1_spmd.clone.sunk | while | flops 408977408 | bytes 8783110 | solution.py:85
  75.6 6.2 %fusion.231 = f32[16,32768]{1,0:T(8,128)} fusion(f32[16,32768]{1,0:T(8,128)} %get-tuple-element.1416, s32[]{:T(128)S(6)} %select_n.80, f32[4,1024,1024]{2,1,0:T(8,128)} %get-tuple-element.1428, s32[]{:T(128)S(6)} %copy.29, pred[]{:T(512)} %bitcast.292, f32[16,32768]{1,0:T(8,128)S(1)} %get-tuple-element.1427, s32[]{:T(128)S(6)} %select_n.81), kind=kOutput, calls=%fused_computation.21.clone.1 | convolution fusion | flops 204488704 | bytes 4391436 | tf_op jit(solution)/shard_map/while/body/eval_jaxpr/dot_general | solution.py:63
  81.8 5.1 fusion.232
  90.0 6.2 %fusion.231 = f32[16,32768]{1,0:T(8,128)} fusion(f32[16,32768]{1,0:T(8,128)} %get-tuple-element.1416, s32[]{:T(128)S(6)} %select_n.80, f32[4,1024,1024]{2,1,0:T(8,128)} %get-tuple-element.1428, s32[]{:T(128)S(6)} %copy.29, pred[]{:T(512)} %bitcast.292, f32[16,32768]{1,0:T(8,128)S(1)} %get-tuple-element.1427, s32[]{:T(128)S(6)} %select_n.81), kind=kOutput, calls=%fused_computation.21.clone.1 | convolution fusion | flops 204488704 | bytes 4391436 | tf_op jit(solution)/shard_map/while/body/eval_jaxpr/dot_general | solution.py:63
  96.2 5.1 fusion.232
  104.5 6.2 %fusion.231 = f32[16,32768]{1,0:T(8,128)} fusion(f32[16,32768]{1,0:T(8,128)} %get-tuple-element.1416, s32[]{:T(128)S(6)} %select_n.80, f32[4,1024,1024]{2,1,0:T(8,128)} %get-tuple-element.1428, s32[]{:T(128)S(6)} %copy.29, pred[]{:T(512)} %bitcast.292, f32[16,32768]{1,0:T(8,128)S(1)} %get-tuple-element.1427, s32[]{:T(128)S(6)} %select_n.81), kind=kOutput, calls=%fused_computation.21.clone.1 | convolution fusion | flops 204488704 | bytes 4391436 | tf_op jit(solution)/shard_map/while/body/eval_jaxpr/dot_general | solution.py:63
  110.7 5.1 fusion.232
  118.9 6.2 %fusion.231 = f32[16,32768]{1,0:T(8,128)} fusion(f32[16,32768]{1,0:T(8,128)} %get-tuple-element.1416, s32[]{:T(128)S(6)} %select_n.80, f32[4,1024,1024]{2,1,0:T(8,128)} %get-tuple-element.1428, s32[]{:T(128)S(6)} %copy.29, pred[]{:T(512)} %bitcast.292, f32[16,32768]{1,0:T(8,128)S(1)} %get-tuple-element.1427, s32[]{:T(128)S(6)} %select_n.81), kind=kOutput, calls=%fused_computation.21.clone.1 | convolution fusion | flops 204488704 | bytes 4391436 | tf_op jit(solution)/shard_map/while/body/eval_jaxpr/dot_general | solution.py:63
  125.1 5.1 fusion.232
  130.3 60.8 %all-reduce.5.cloned.1.call-done = f32[16,32768]{1,0:T(8,128)} async-done(((f32[16,32768]{1,0:T(8,128)}), f32[16,32768]{1,0:T(8,128)}) %all-reduce.5.cloned.1.call-update) | async-done | bytes 2097168 | tf_op jit(solution)/shard_map/psum | solution.py:10
  191.2 42.0 %all_gather.7 = f32[32768]{0:T(1024)S(1)} all-gather(f32[1024]{0:T(1024)S(1)} %copy-done.5), channel_id=1, replica_groups=mesh['grp'=4,'tile'=8] {'grp','tile'}, dimensions={0}, use_global_device_ids=true | all-gather | bytes 135168 | tf_op jit(solution)/shard_map/all_gather | solution.py:93
  233.1 2.9 fusion.110
  237.4 41.9 %all-reduce.7.cloned.1.call-done = f32[16,32768]{1,0:T(8,128)} async-done(((f32[16,32768]{1,0:T(8,128)}), f32[16,32768]{1,0:T(8,128)}) %all-reduce.7.cloned.1.call-update) | async-done | bytes 2097168 | tf_op jit(solution)/shard_map/psum | solution.py:11
  279.3 4.5 fusion.55
  285.3 0.6 slice.2233
  286.8 0.6 slice.2171
  288.4 0.6 slice.2175
  290.0 0.6 slice.2179
  291.6 0.6 slice.2183
  293.3 0.6 slice.2187
  294.9 0.6 slice.2191
  296.5 0.6 slice.2195
  298.1 0.6 slice.2199
  299.7 0.6 slice.2203
  301.4 0.6 slice.2207
  303.0 0.6 slice.2211
  304.8 0.6 slice.2215
  306.4 0.6 slice.2219
  308.0 0.6 slice.2223
  309.7 0.6 slice.2227
  311.3 3.6 convolution_subtract_fusion
  314.8 2.9 fusion.112
  341.0 4.3 convolution_add_fusion
  345.3 1.5 broadcast.1560
  346.8 58.0 %while.116 = (s32[]{:T(128)}, f32[16,32768]{1,0:T(8,128)}, s32[4,2]{0,1:T(2,128)S(1)}, f32[16,32768]{1,0:T(8,128)}, f32[4,1024,1024]{2,1,0:T(8,128)}, /*index=5*/s32[]{:T(128)}, s32[1,1]{0,1:T(1,128)}, s32[]{:T(128)}, s32[]{:T(128)}) while((s32[]{:T(128)}, f32[16,32768]{1,0:T(8,128)}, s32[4,2]{0,1:T(2,128)S(1)}, ...), condition=%wide.region_5.6_spmd.clone, body=%wide.region_4.5_spmd.clone.sunk | while | flops 408977408 | bytes 8783110 | solution.py:85
  350.0 6.2 %fusion.236 = f32[16,32768]{1,0:T(8,128)} fusion(f32[16,32768]{1,0:T(8,128)} %get-tuple-element.1443, s32[]{:T(128)S(6)} %select_n.84, f32[4,1024,1024]{2,1,0:T(8,128)} %get-tuple-element.1455, s32[]{:T(128)S(6)} %copy.99, pred[]{:T(512)} %bitcast.297, f32[16,32768]{1,0:T(8,128)} %get-tuple-element.1454, s32[]{:T(128)S(6)} %select_n.85), kind=kOutput, calls=%fused_computation.46.clone.1 | convolution fusion | flops 204488704 | bytes 4391436 | tf_op jit(solution)/shard_map/while/body/eval_jaxpr/dot_general | solution.py:63
  356.2 5.1 fusion.237
  364.5 6.2 %fusion.236 = f32[16,32768]{1,0:T(8,128)} fusion(f32[16,32768]{1,0:T(8,128)} %get-tuple-element.1443, s32[]{:T(128)S(6)} %select_n.84, f32[4,1024,1024]{2,1,0:T(8,128)} %get-tuple-element.1455, s32[]{:T(128)S(6)} %copy.99, pred[]{:T(512)} %bitcast.297, f32[16,32768]{1,0:T(8,128)} %get-tuple-element.1454, s32[]{:T(128)S(6)} %select_n.85), kind=kOutput, calls=%fused_computation.46.clone.1 | convolution fusion | flops 204488704 | bytes 4391436 | tf_op jit(solution)/shard_map/while/body/eval_jaxpr/dot_general | solution.py:63
  370.7 5.1 fusion.237
  379.0 6.2 %fusion.236 = f32[16,32768]{1,0:T(8,128)} fusion(f32[16,32768]{1,0:T(8,128)} %get-tuple-element.1443, s32[]{:T(128)S(6)} %select_n.84, f32[4,1024,1024]{2,1,0:T(8,128)} %get-tuple-element.1455, s32[]{:T(128)S(6)} %copy.99, pred[]{:T(512)} %bitcast.297, f32[16,32768]{1,0:T(8,128)} %get-tuple-element.1454, s32[]{:T(128)S(6)} %select_n.85), kind=kOutput, calls=%fused_computation.46.clone.1 | convolution fusion | flops 204488704 | bytes 4391436 | tf_op jit(solution)/shard_map/while/body/eval_jaxpr/dot_general | solution.py:63
  385.2 5.1 fusion.237
  393.5 6.2 %fusion.236 = f32[16,32768]{1,0:T(8,128)} fusion(f32[16,32768]{1,0:T(8,128)} %get-tuple-element.1443, s32[]{:T(128)S(6)} %select_n.84, f32[4,1024,1024]{2,1,0:T(8,128)} %get-tuple-element.1455, s32[]{:T(128)S(6)} %copy.99, pred[]{:T(512)} %bitcast.297, f32[16,32768]{1,0:T(8,128)} %get-tuple-element.1454, s32[]{:T(128)S(6)} %select_n.85), kind=kOutput, calls=%fused_computation.46.clone.1 | convolution fusion | flops 204488704 | bytes 4391436 | tf_op jit(solution)/shard_map/while/body/eval_jaxpr/dot_general | solution.py:63
  399.7 5.1 fusion.237
  404.8 60.8 %all-reduce.9.cloned.1.call-done = f32[16,32768]{1,0:T(8,128)} async-done(((f32[16,32768]{1,0:T(8,128)}), f32[16,32768]{1,0:T(8,128)}) %all-reduce.9.cloned.1.call-update) | async-done | bytes 2097168 | tf_op jit(solution)/shard_map/psum | solution.py:10
  465.7 3.2 fusion.111
  469.0 84.2 %all-reduce.11.cloned.1.call-done = f32[16,32768]{1,0:T(8,128)} async-done(((f32[16,32768]{1,0:T(8,128)}), f32[16,32768]{1,0:T(8,128)}) %all-reduce.11.cloned.1.call-update) | async-done | bytes 2097168 | tf_op jit(solution)/shard_map/psum | solution.py:11
  553.1 5.8 fusion.54
  560.4 0.6 slice.2295
  563.7 0.6 slice.2303
  565.4 0.6 slice.2307
  567.0 0.6 slice.2311
  568.7 0.6 slice.2315
  570.4 0.6 slice.2319
  573.7 0.6 slice.2327
  575.3 0.6 slice.2331
  577.2 0.6 slice.2335
  585.4 1.9 fusion.113
  587.4 2.0 fusion.53
  589.4 1.5 dynamic-slice_subtract_fusion
  590.9 1.5 dynamic-slice_add_fusion
  (429 shorter events, 35.0 us)
Async XLA Ops:
  7.2 64.4 %copy-start.4 = (s32[4,2]{0,1:T(2,128)S(1)}, s32[4,2]{0,1:T(2,128)}, u32[]{:S(2)}) copy-start(s32[4,2]{0,1:T(2,128)} %param.197) | copy-start | bytes 100
  7.2 62.9 %all-gather.2.cloned.1.call-start = ((), (), s32[]{:S(2)}) async-start(), calls=%async_computation | async-start | bytes 2162688 | tf_op jit(solution)/shard_map/all_gather | solution.py:92
  7.9 183.2 %all-reduce.5.cloned.1.call-start = ((), (), s32[]{:S(2)}) async-start(), calls=%async_computation.1 | async-start | bytes 4194304 | tf_op jit(solution)/shard_map/psum | solution.py:10
  70.1 2.3 copy-start
  130.2 61.0 %copy-start.5 = (f32[1024]{0:T(1024)S(1)}, f32[1024]{0:T(1024)}, u32[]{:S(2)}) copy-start(f32[1024]{0:T(1024)} %param.195) | copy-start | bytes 12292
  130.2 149.1 %all-reduce.7.cloned.1.call-start = ((), (), s32[]{:S(2)}) async-start(), calls=%async_computation.2 | async-start | bytes 4194304 | tf_op jit(solution)/shard_map/psum | solution.py:11
  191.1 274.6 %all-reduce.9.cloned.1.call-start = ((), (), s32[]{:S(2)}) async-start(), calls=%async_computation.3 | async-start | bytes 4194304 | tf_op jit(solution)/shard_map/psum | solution.py:10
  314.8 2.9 copy-start.2
  404.8 148.3 %all-reduce.11.cloned.1.call-start = ((), (), s32[]{:S(2)}) async-start(), calls=%async_computation.4 | async-start | bytes 4194304 | tf_op jit(solution)/shard_map/psum | solution.py:11
  553.1 32.3 %copy-start.1 = (f32[16,32768]{1,0:T(8,128)S(1)}, f32[16,32768]{1,0:T(8,128)}, u32[]{:S(2)}) copy-start(f32[16,32768]{1,0:T(8,128)} %get-tuple-element.1467) | copy-start | bytes 6291460
  585.4 1.9 copy-start.3
Sparse Core Ops, SparseCore 0:
  10.9 59.1 all-gather.1
  130.4 60.6 all-reduce.4
  193.5 85.7 all-reduce.6
  404.9 60.7 all-reduce.8
  467.9 85.1 all-reduce.10
